TPU v7x, 32 devices: a whole 2x2x4 slice. The times are simulated.
32 devices in a mesh: pb: 8 (over y, x, core), row: 4 (over z).
Axes of the slice: x: 2, y: 2, z: 4, core: 2. Of those that a mesh axis runs over, the one named last changes fastest.
Arguments:
- valence_bands: bfloat16 [8, 20, 4096], P('pb', None, 'row'), may hold values from -0.75 to 0.75
- conduction_bands: bfloat16 [8, 20, 4096], P('pb', None, 'row'), may hold values from -6 to 6
- screened: bfloat16 [8, 4096, 4096], P('pb', 'row'), may hold values from -0.09375 to 0.09375
- pair_list: int32 [16, 2], replicated, may hold values from 0 to 7, as said below
- transfer_index: int32 [16, 1], replicated, may hold values from 0 to 7; in each aligned block of 16 rows (0 to 15, 16 to 31, ...) at most 6 rows name the same one
- owner_map: int32 [8], replicated, may hold values from 0 to 7, as said below
Outputs:
- direct: bfloat16 [16, 400, 400], P('pb', 'row')
- mirror: bfloat16 [16, 400, 400], P('pb', 'row')
Inputs may be any that keep to these rules, and one draw needn't show every extreme that they name: owner_map is a permutation of 0 to 7. `pair_list`: the two k-points of a pair differ. The first k-point of pairs e * 2 to e * 2 + 1 is the one that owner_map sends to e. Over all pairs, the second k-points are sent by owner_map to every value 0 to 7 exactly 2 times. `transfer_index`: at most 6 pairs share one momentum transfer, and some transfer has exactly 6; every transfer has at least one pair.
All inputs are finite; a program needn't handle non-finite values.
Results may differ from a plain program's by a relative error of at most 0.0065.
Values may be sent and summed in bfloat16 or wider, within the bound.
No kernel may reach another device: no remote copies, remote signals or barrier semaphores. Data moves between devices by JAX's collectives and lax.ppermute only.
A program may use at most 64 MiB of HBM per device.

v0:
```python
import jax
import jax.numpy as jnp
from jax import lax
from jax.sharding import PartitionSpec as P

PAIR_DEV = 2
MOST = 6


def rank_table(labels, groups, slots_per):
    total_rows = labels.shape[0]
    member = (labels[None, :] == jnp.arange(groups, dtype=jnp.int32)[:, None]).astype(jnp.int32)
    before = jnp.cumsum(member, axis=1) - 1
    placed = member[:, None, :] * (
        before[:, None, :] == jnp.arange(slots_per, dtype=jnp.int32)[None, :, None]
    ).astype(jnp.int32)
    numbers = jnp.arange(total_rows, dtype=jnp.int32) + 1
    return jnp.sum(placed * numbers[None, None, :], axis=2) - 1


def pair_kernel(val_first, val_second, con_first, con_second, screen_rows):
    val_count = val_first.shape[0]
    con_count = con_first.shape[0]
    val_pairs = val_first[:, None, :].astype(jnp.float32) * val_second[None, :, :].astype(
        jnp.float32
    )
    val_pairs = val_pairs.reshape(val_count * val_count, val_first.shape[1]).astype(jnp.bfloat16)
    con_pairs = con_first[:, None, :].astype(jnp.float32) * con_second[None, :, :].astype(
        jnp.float32
    )
    con_pairs = con_pairs.reshape(con_count * con_count, con_first.shape[1]).astype(jnp.bfloat16)
    interim = lax.dot_general(
        screen_rows, con_pairs, (((1,), (1,)), ((), ())), preferred_element_type=jnp.float32
    ).astype(jnp.bfloat16)
    partial_sum = jnp.dot(val_pairs, interim, preferred_element_type=jnp.float32)
    partial_sum = partial_sum.reshape(val_count, val_count, con_count, con_count).transpose(
        0, 2, 1, 3
    )
    return partial_sum.reshape(val_count * con_count, val_count * con_count)


def shards(valence_bands, conduction_bands, screened, pair_list, transfer_index, owner_map):
    groups = lax.axis_size("pb")
    rows_split = lax.axis_size("row")
    device = lax.axis_index("pb")
    val_all, con_local = (
        lax.all_gather(valence_bands, "pb", axis=0, tiled=True),
        lax.all_gather(conduction_bands, "pb", axis=0, tiled=True),
    )
    slot_table = rank_table(transfer_index[:, 0], groups, MOST)
    own_slots = lax.dynamic_index_in_dim(slot_table, device, 0, keepdims=False)
    live_pair = jnp.maximum(own_slots, 0)
    slot_first = jnp.take(owner_map, jnp.take(pair_list[:, 0], live_pair))
    slot_second = jnp.take(owner_map, jnp.take(pair_list[:, 1], live_pair))
    val_first = jnp.take(val_all, slot_first, axis=0)
    val_second = jnp.take(val_all, slot_second, axis=0)
    con_full = lax.all_gather(con_local, "row", axis=2, tiled=True)
    con_first = jnp.take(con_full, slot_first, axis=0)
    con_second = jnp.take(con_full, slot_second, axis=0)
    screen_rows = screened[0]

    def one_slot(operands):
        return pair_kernel(operands[0], operands[1], operands[2], operands[3], screen_rows)

    partials = lax.map(one_slot, (val_first, val_second, con_first, con_second))
    shares = lax.psum_scatter(partials, "row", scatter_dimension=1, tiled=True).astype(jnp.bfloat16)
    band_rows = shares.shape[1]
    mirror_table = rank_table(jnp.take(owner_map, pair_list[:, 1]), groups, PAIR_DEV)
    flat_slots = slot_table.reshape(-1)
    own_direct = device * PAIR_DEV + jnp.arange(PAIR_DEV, dtype=jnp.int32)
    own_mirror = lax.dynamic_index_in_dim(mirror_table, device, 0, keepdims=False)
    wanted = jnp.concatenate([own_direct, own_mirror])
    select = (wanted[:, None] == flat_slots[None, :]).astype(jnp.bfloat16)
    arrived = jnp.einsum(
        "ji,ixy->jxy",
        select,
        lax.all_gather(shares, "pb", axis=0, tiled=True),
        preferred_element_type=jnp.float32,
    )
    direct = arrived[:PAIR_DEV].astype(jnp.bfloat16)
    mirror_rows = arrived[PAIR_DEV:].astype(jnp.bfloat16)
    turned = jnp.transpose(mirror_rows, (0, 2, 1)).reshape(
        PAIR_DEV, rows_split, band_rows, band_rows
    )
    swapped = lax.all_to_all(turned, "row", split_axis=1, concat_axis=3, tiled=True)
    mirror = swapped.reshape(PAIR_DEV, band_rows, band_rows * rows_split)
    return (direct, mirror)


def solution(mesh):
    in_specs = (P("pb", None, "row"), P("pb", None, "row"), P("pb", "row", None), P(), P(), P())
    out_specs = (P("pb", "row", None), P("pb", "row", None))
    return jax.shard_map(shards, mesh=mesh, in_specs=in_specs, out_specs=out_specs, check_vma=False)
```

profile of v0, /device:TPU:0, one launch (start us, length us, event | category | flops | bytes accessed | tf_op | source)
XLA Modules:
  0.0 460.9 jit_solution(9152695233821279163)
XLA Ops:
  7.2 12.9 %all_gather.13 = bf16[8,20,1024]{2,1,0:T(8,128)(2,1)} all-gather(bf16[1,20,1024]{2,1,0:T(8,128)(2,1)} %param.17), channel_id=1, replica_groups=mesh['pb'=8,'row'=4] {'pb'}, dimensions={0}, use_global_device_ids=true | all-gather | bytes 368640 | tf_op jit(solution)/shard_map/all_gather | solution.py:48
  24.9 8.8 %all_gather.12 = bf16[8,20,1024]{2,1,0:T(8,128)(2,1)S(1)} all-gather(bf16[1,20,1024]{2,1,0:T(8,128)(2,1)} %param.16), channel_id=1, replica_groups=mesh['pb'=8,'row'=4] {'pb'}, dimensions={0}, use_global_device_ids=true | all-gather | bytes 368640 | tf_op jit(solution)/shard_map/all_gather | solution.py:47
  37.8 19.8 %all-gather.3.cloned.1.call-done = bf16[8,20,4096]{2,1,0:T(8,128)(2,1)} async-done(((bf16[8,20,1024]{2,1,0:T(8,128)(2,1)}), bf16[8,20,4096]{2,1,0:T(8,128)(2,1)}) %all-gather.3.cloned.1.call-update) | async-done | bytes 1310736 | tf_op jit(solution)/shard_map/all_gather | solution.py:57
  62.8 156.2 %while.10 = (s32[]{:T(128)}, f32[6,400,400]{1,2,0:T(8,128)}, bf16[6,20,1024]{2,1,0:T(8,128)(2,1)}, bf16[6,20,1024]{2,1,0:T(8,128)(2,1)}, bf16[6,20,4096]{2,1,0:T...) while((s32[]{:T(128)}, f32[6,400,400]{1,2,0:T(8,128)}, ...), condition=%wide.region_5.10_spmd, body=%wide.region_4.9_spmd.sunk | while | flops 3687833600 | bytes 31480412 | solution.py:65
  66.5 3.9 convert_element_type.89
  70.4 7.0 %convolution_convert_fusion.3 = bf16[400,1024]{1,0:T(8,128)(2,1)} fusion(bf16[400,4096]{1,0:T(8,128)(2,1)S(1)} %convert_element_type.89, bf16[1024,4096]{1,0:T(8,128)(2,1)} %get-tuple-element.156), kind=kOutput, calls=%fused_computation.12.clone.1 | convolution fusion | flops 3355852800 | bytes 12484608 | tf_op jit(solution)/shard_map/while/body/eval_jaxpr/dot_general | solution.py:32
  79.5 4.5 convolution_bitcast_fusion.2
  92.6 3.9 convert_element_type.89
  96.4 7.0 %convolution_convert_fusion.3 = bf16[400,1024]{1,0:T(8,128)(2,1)} fusion(bf16[400,4096]{1,0:T(8,128)(2,1)S(1)} %convert_element_type.89, bf16[1024,4096]{1,0:T(8,128)(2,1)} %get-tuple-element.156), kind=kOutput, calls=%fused_computation.12.clone.1 | convolution fusion | flops 3355852800 | bytes 12484608 | tf_op jit(solution)/shard_map/while/body/eval_jaxpr/dot_general | solution.py:32
  105.6 4.5 convolution_bitcast_fusion.2
  118.6 3.9 convert_element_type.89
  122.5 7.0 %convolution_convert_fusion.3 = bf16[400,1024]{1,0:T(8,128)(2,1)} fusion(bf16[400,4096]{1,0:T(8,128)(2,1)S(1)} %convert_element_type.89, bf16[1024,4096]{1,0:T(8,128)(2,1)} %get-tuple-element.156), kind=kOutput, calls=%fused_computation.12.clone.1 | convolution fusion | flops 3355852800 | bytes 12484608 | tf_op jit(solution)/shard_map/while/body/eval_jaxpr/dot_general | solution.py:32
  131.6 4.5 convolution_bitcast_fusion.2
  144.6 3.9 convert_element_type.89
  148.5 7.0 %convolution_convert_fusion.3 = bf16[400,1024]{1,0:T(8,128)(2,1)} fusion(bf16[400,4096]{1,0:T(8,128)(2,1)S(1)} %convert_element_type.89, bf16[1024,4096]{1,0:T(8,128)(2,1)} %get-tuple-element.156), kind=kOutput, calls=%fused_computation.12.clone.1 | convolution fusion | flops 3355852800 | bytes 12484608 | tf_op jit(solution)/shard_map/while/body/eval_jaxpr/dot_general | solution.py:32
  157.6 4.5 convolution_bitcast_fusion.2
  174.5 7.0 %convolution_convert_fusion.3 = bf16[400,1024]{1,0:T(8,128)(2,1)} fusion(bf16[400,4096]{1,0:T(8,128)(2,1)S(1)} %convert_element_type.89, bf16[1024,4096]{1,0:T(8,128)(2,1)} %get-tuple-element.156), kind=kOutput, calls=%fused_computation.12.clone.1 | convolution fusion | flops 3355852800 | bytes 12484608 | tf_op jit(solution)/shard_map/while/body/eval_jaxpr/dot_general | solution.py:32
  183.7 4.5 convolution_bitcast_fusion.2
  200.5 7.0 %convolution_convert_fusion.3 = bf16[400,1024]{1,0:T(8,128)(2,1)} fusion(bf16[400,4096]{1,0:T(8,128)(2,1)S(1)} %convert_element_type.89, bf16[1024,4096]{1,0:T(8,128)(2,1)} %get-tuple-element.156), kind=kOutput, calls=%fused_computation.12.clone.1 | convolution fusion | flops 3355852800 | bytes 12484608 | tf_op jit(solution)/shard_map/while/body/eval_jaxpr/dot_general | solution.py:32
  209.7 4.5 convolution_bitcast_fusion.2
  219.0 169.8 %all-reduce.2 = bf16[6,400,400]{1,2,0:T(8,128)(2,1)S(1)} all-reduce(f32[6,400,400]{1,2,0:T(8,128)} %get-tuple-element.43), channel_id=2, replica_groups=mesh['pb'=8,'row'=4] {'row'}, use_global_device_ids=true, to_apply=%region_6.11.clone | all-reduce | flops 960000 | bytes 5760000
  391.4 36.1 %all-gather.5.cloned.1.call-done = bf16[48,100,400]{1,2,0:T(8,128)(2,1)} async-done(((bf16[6,100,400]{1,2,0:T(8,128)(2,1)}), bf16[48,100,400]{1,2,0:T(8,128)(2,1)}) %all-gather.5.cloned.1.call-update) | async-done | bytes 3840016 | tf_op jit(solution)/shard_map/all_gather | solution.py:77
  427.5 8.4 %copy.27 = bf16[48,100,400]{2,0,1:T(8,128)(2,1)} copy(bf16[48,100,400]{1,2,0:T(8,128)(2,1)} %all-gather.5.cloned.1.call-done) | data formatting | bytes 7680000 | tf_op jit(solution)/shard_map/all_gather | solution.py:77
  440.4 12.5 %all_to_all.15 = bf16[2,4,100,100]{2,0,3,1:T(2,128)(2,1)S(1)} all-to-all(bf16[2,4,100,100]{2,0,3,1:T(2,128)(2,1)S(1)} %copy.28), channel_id=1, replica_groups=mesh['pb'=8,'row'=4] {'row'}, dimensions={1} | all-to-all | bytes 320000 | tf_op jit(solution)/shard_map/all_to_all | solution.py:85
  (105 shorter events, 93.0 us)
Async XLA Ops:
  7.2 16.4 %copy-start = (s32[8]{0:T(128)S(1)}, s32[8]{0:T(128)}, u32[]{:S(2)}) copy-start(s32[8]{0:T(128)} %param.21) | copy-start | bytes 100
  7.2 27.8 %copy-start.3 = (u32[32]{0:T(128)S(1)}, u32[32]{0:T(128)}, u32[]{:S(2)}) copy-start(u32[32]{0:T(128)} %constant.110) | copy-start | bytes 388
  7.2 50.4 %all-gather.3.cloned.1.call-start = ((), (), s32[]{:S(2)}) async-start(), calls=%async_computation.1 | async-start | bytes 1966080 | tf_op jit(solution)/shard_map/all_gather | solution.py:57
  20.2 407.3 %all-gather.5.cloned.1.call-start = ((), (), s32[]{:S(2)}) async-start(), calls=%async_computation.2 | async-start | bytes 5529600 | tf_op jit(solution)/shard_map/all_gather | solution.py:77
  57.6 3.4 copy-start.1
  219.0 171.7 %copy-start.2 = (s32[16,2]{0,1:T(2,128)S(1)}, s32[16,2]{0,1:T(2,128)}, u32[]{:S(2)}) copy-start(s32[16,2]{0,1:T(2,128)} %param.19) | copy-start | bytes 388
Sparse Core Ops, SparseCore 0:
  20.3 37.2 all-gather.2
  390.1 37.3 all-gather.4
where the time goes:
time: 463 us; the launch traced here: 461 us
  blocking collectives  204 us (44%)
  local copies, waits for them, and re-layouts  80 us (17%)
  matrix products  72.2 us (16%)
  waiting for transfers between devices  55.9 us (12%)
  other arithmetic  33.6 us (7%)
  between operations  14.9 us (3%)
    unnamed x1, blocking collectives  170 us
    dot_general x6, matrix products, pair_kernel(): lax.dot_general(screen_rows, con_pairs, (((1,), (1,)), ((), ())), preferr...  42.1 us
    all_gather x1, waiting for transfers between devices, shards(): lax.all_gather(shares, 'pb', axis=0, tiled=True)  36.1 us
    dot_general x6, matrix products, pair_kernel(): jnp.dot(val_pairs, interim, preferred_element_type=jnp.float32)  26.8 us
    convert_element_type x6, local copies, waits for them, and re-layouts, pair_kernel(): con_pairs.reshape(con_count * con_count, con_first.shape[1])  23.3 us
    broadcast_in_dim x6, local copies, waits for them, and re-layouts, shards(): partials = lax.map(one_slot, (val_first, val_second, con_first, con_second))  21.6 us
    all_gather x1, waiting for transfers between devices, shards(): con_full = lax.all_gather(con_local, 'row', axis=2, tiled=True)  19.8 us
    convert_element_type x6, other arithmetic, pair_kernel(): con_pairs.reshape(con_count * con_count, con_first.shape[1])  15.6 us
  transfers between devices with their start and end apart: 2, of which 2 were waited for; matrix products, arithmetic and copies ran while one was open for 2% of the time, Pallas kernels for 0%

commit v1 on v0

--- a/solution.py
+++ b/solution.py
@@ -40,6 +40,29 @@
 
 
 def shards(valence_bands, conduction_bands, screened, pair_list, transfer_index, owner_map):
+
+    def extend_matrix_here(chunk, z_in):
+        a_name = "pb"
+        spare, arr_next, high = (
+            jax.lax.axis_size(a_name),
+            jax.lax.axis_index(a_name),
+            chunk.shape[0],
+        )
+        by_place = list(map(lambda p: (p, (p + 1) % spare), range(spare)))
+        series = list(map(lambda p: (p, (p - 1) % spare), range(spare)))
+        heard = spare // 2
+        e_next = ready = chunk
+        block_last = z_in(chunk, arr_next * high)
+        ix = 1
+        while ix < heard + 1:
+            e_next = jax.lax.ppermute(e_next, a_name, perm=by_place)
+            if ix < spare - heard:
+                ready = jax.lax.ppermute(ready, a_name, perm=series)
+                block_last = block_last + z_in(ready, (arr_next + ix) % spare * high)
+            block_last = block_last + z_in(e_next, (arr_next - ix) % spare * high)
+            ix += 1
+        return block_last
+
     groups = lax.axis_size("pb")
     rows_split = lax.axis_size("row")
     device = lax.axis_index("pb")
@@ -71,11 +94,14 @@
     own_mirror = lax.dynamic_index_in_dim(mirror_table, device, 0, keepdims=False)
     wanted = jnp.concatenate([own_direct, own_mirror])
     select = (wanted[:, None] == flat_slots[None, :]).astype(jnp.bfloat16)
-    arrived = jnp.einsum(
-        "ji,ixy->jxy",
-        select,
-        lax.all_gather(shares, "pb", axis=0, tiled=True),
-        preferred_element_type=jnp.float32,
+    arrived = extend_matrix_here(
+        shares,
+        lambda own_block, offset: jnp.einsum(
+            "ji,ixy->jxy",
+            lax.dynamic_slice_in_dim(select, offset, own_block.shape[0], axis=1),
+            own_block,
+            preferred_element_type=jnp.float32,
+        ),
     )
     direct = arrived[:PAIR_DEV].astype(jnp.bfloat16)
     mirror_rows = arrived[PAIR_DEV:].astype(jnp.bfloat16)

time: 463 us -> 478 us (1.032)
  starting transfers between devices: 0.08 us -> 6.3 us
  waiting for transfers between devices: 55.9 us -> 62.1 us
  local copies, waits for them, and re-layouts: 80 us -> 86.1 us
    ppermute x0 -> x7, waiting for transfers between devices: none -> 43.5 us  [the longest x4 43.5 us: extend_matrix_here(): e_next = jax.lax.ppermute(e_next, a_name, perm=by_place)]
    all_gather x1 -> x0, waiting for transfers between devices: 36.1 us -> none  [shards(): lax.all_gather(shares, 'pb', axis=0, tiled=True)]
    ppermute x0 -> x7, local copies, waits for them, and re-layouts: none -> 14.1 us  [the longest x4 8.58 us: extend_matrix_here(): e_next = jax.lax.ppermute(e_next, a_name, perm=by_place)]
    all_gather x1 -> x0, local copies, waits for them, and re-layouts: 8.41 us -> none  [shards(): lax.all_gather(shares, 'pb', axis=0, tiled=True)]
    ppermute x0 -> x7, starting transfers between devices: none -> 6.26 us  [the longest x3 5.41 us: extend_matrix_here(): ready = jax.lax.ppermute(ready, a_name, perm=series)]
  transfers between devices with their start and end apart: 2 -> 8, of which waited for: 2 -> 5; matrix products, arithmetic and copies ran while one was open for 2% -> 5% of each run, Pallas kernels for 0% -> 0%
where the time goes in v1:
time: 478 us; the launch traced here: 476 us
  blocking collectives  201 us (42%)
  local copies, waits for them, and re-layouts  86.1 us (18%)
  matrix products  72.4 us (15%)
  waiting for transfers between devices  62.1 us (13%)
  other arithmetic  33.8 us (7%)
  between operations  15.1 us (3%)
  starting transfers between devices  6.3 us (1%)
    unnamed x1, blocking collectives  170 us
    ppermute x4, waiting for transfers between devices, extend_matrix_here(): e_next = jax.lax.ppermute(e_next, a_name, perm=by_place)  43.5 us
    dot_general x6, matrix products, pair_kernel(): lax.dot_general(screen_rows, con_pairs, (((1,), (1,)), ((), ())), preferr...  42.1 us
    dot_general x6, matrix products, pair_kernel(): jnp.dot(val_pairs, interim, preferred_element_type=jnp.float32)  26.7 us
    convert_element_type x6, local copies, waits for them, and re-layouts, pair_kernel(): con_pairs.reshape(con_count * con_count, con_first.shape[1])  23.3 us
    broadcast_in_dim x6, local copies, waits for them, and re-layouts, shards(): partials = lax.map(one_slot, (val_first, val_second, con_first, con_second))  21.6 us
    all_gather x1, waiting for transfers between devices, shards(): con_full = lax.all_gather(con_local, 'row', axis=2, tiled=True)  18.5 us
    convert_element_type x6, other arithmetic, pair_kernel(): con_pairs.reshape(con_count * con_count, con_first.shape[1])  15.7 us
  transfers between devices with their start and end apart: 8, of which 5 were waited for; matrix products, arithmetic and copies ran while one was open for 5% of the time, Pallas kernels for 0%

profile of v1, /device:TPU:0, one launch (start us, length us, event | category | flops | bytes accessed | tf_op | source)
XLA Modules:
  0.0 476.5 jit_solution(12604587060664882049)
XLA Ops:
  7.2 12.9 %all_gather.10 = bf16[8,20,1024]{2,1,0:T(8,128)(2,1)} all-gather(bf16[1,20,1024]{2,1,0:T(8,128)(2,1)} %param.17), channel_id=1, replica_groups=mesh['pb'=8,'row'=4] {'pb'}, dimensions={0}, use_global_device_ids=true | all-gather | bytes 368640 | tf_op jit(solution)/shard_map/all_gather | solution.py:71
  24.9 8.7 %all_gather.9 = bf16[8,20,1024]{2,1,0:T(8,128)(2,1)S(1)} all-gather(bf16[1,20,1024]{2,1,0:T(8,128)(2,1)S(1)} %copy-done.2), channel_id=1, replica_groups=mesh['pb'=8,'row'=4] {'pb'}, dimensions={0}, use_global_device_ids=true | all-gather | bytes 368640 | tf_op jit(solution)/shard_map/all_gather | solution.py:70
  39.1 18.5 %all-gather.2.cloned.1.call-done = bf16[8,20,4096]{2,1,0:T(8,128)(2,1)} async-done(((bf16[8,20,1024]{2,1,0:T(8,128)(2,1)}), bf16[8,20,4096]{2,1,0:T(8,128)(2,1)}) %all-gather.2.cloned.1.call-update) | async-done | bytes 1310736 | tf_op jit(solution)/shard_map/all_gather | solution.py:80
  62.8 156.1 %while.10 = (s32[]{:T(128)}, f32[6,400,400]{1,2,0:T(8,128)}, bf16[6,20,1024]{2,1,0:T(8,128)(2,1)}, bf16[6,20,1024]{2,1,0:T(8,128)(2,1)}, bf16[6,20,4096]{2,1,0:T...) while((s32[]{:T(128)}, f32[6,400,400]{1,2,0:T(8,128)}, ...), condition=%wide.region_5.10_spmd, body=%wide.region_4.9_spmd.sunk | while | flops 3687833600 | bytes 31480412 | solution.py:88
  70.4 7.0 %convolution_convert_fusion.2 = bf16[400,1024]{1,0:T(8,128)(2,1)} fusion(bf16[400,4096]{1,0:T(8,128)(2,1)S(1)} %convert_element_type.89, bf16[1024,4096]{1,0:T(8,128)(2,1)} %get-tuple-element.156), kind=kOutput, calls=%fused_computation.12.clone.1 | convolution fusion | flops 3355852800 | bytes 12484608 | tf_op jit(solution)/shard_map/while/body/eval_jaxpr/dot_general | solution.py:32
  79.5 4.4 convolution_bitcast_fusion.2
  96.4 7.0 %convolution_convert_fusion.2 = bf16[400,1024]{1,0:T(8,128)(2,1)} fusion(bf16[400,4096]{1,0:T(8,128)(2,1)S(1)} %convert_element_type.89, bf16[1024,4096]{1,0:T(8,128)(2,1)} %get-tuple-element.156), kind=kOutput, calls=%fused_computation.12.clone.1 | convolution fusion | flops 3355852800 | bytes 12484608 | tf_op jit(solution)/shard_map/while/body/eval_jaxpr/dot_general | solution.py:32
  105.5 4.5 convolution_bitcast_fusion.2
  122.4 7.0 %convolution_convert_fusion.2 = bf16[400,1024]{1,0:T(8,128)(2,1)} fusion(bf16[400,4096]{1,0:T(8,128)(2,1)S(1)} %convert_element_type.89, bf16[1024,4096]{1,0:T(8,128)(2,1)} %get-tuple-element.156), kind=kOutput, calls=%fused_computation.12.clone.1 | convolution fusion | flops 3355852800 | bytes 12484608 | tf_op jit(solution)/shard_map/while/body/eval_jaxpr/dot_general | solution.py:32
  131.6 4.4 convolution_bitcast_fusion.2
  144.5 3.9 convert_element_type.89
  148.4 7.0 %convolution_convert_fusion.2 = bf16[400,1024]{1,0:T(8,128)(2,1)} fusion(bf16[400,4096]{1,0:T(8,128)(2,1)S(1)} %convert_element_type.89, bf16[1024,4096]{1,0:T(8,128)(2,1)} %get-tuple-element.156), kind=kOutput, calls=%fused_computation.12.clone.1 | convolution fusion | flops 3355852800 | bytes 12484608 | tf_op jit(solution)/shard_map/while/body/eval_jaxpr/dot_general | solution.py:32
  157.6 4.4 convolution_bitcast_fusion.2
  170.6 3.9 convert_element_type.89
  174.4 7.0 %convolution_convert_fusion.2 = bf16[400,1024]{1,0:T(8,128)(2,1)} fusion(bf16[400,4096]{1,0:T(8,128)(2,1)S(1)} %convert_element_type.89, bf16[1024,4096]{1,0:T(8,128)(2,1)} %get-tuple-element.156), kind=kOutput, calls=%fused_computation.12.clone.1 | convolution fusion | flops 3355852800 | bytes 12484608 | tf_op jit(solution)/shard_map/while/body/eval_jaxpr/dot_general | solution.py:32
  183.6 4.5 convolution_bitcast_fusion.2
  200.5 7.0 %convolution_convert_fusion.2 = bf16[400,1024]{1,0:T(8,128)(2,1)} fusion(bf16[400,4096]{1,0:T(8,128)(2,1)S(1)} %convert_element_type.89, bf16[1024,4096]{1,0:T(8,128)(2,1)} %get-tuple-element.156), kind=kOutput, calls=%fused_computation.12.clone.1 | convolution fusion | flops 3355852800 | bytes 12484608 | tf_op jit(solution)/shard_map/while/body/eval_jaxpr/dot_general | solution.py:32
  209.6 4.5 convolution_bitcast_fusion.2
  218.9 169.8 %all-reduce.2 = bf16[6,400,400]{1,2,0:T(8,128)(2,1)S(1)} all-reduce(f32[6,400,400]{1,2,0:T(8,128)} %get-tuple-element.43), channel_id=2, replica_groups=mesh['pb'=8,'row'=4] {'row'}, use_global_device_ids=true, to_apply=%region_6.11.clone | all-reduce | flops 960000 | bytes 5760000
  391.2 13.9 %collective-permute-done.1 = bf16[6,100,400]{1,2,0:T(8,128)(2,1)} collective-permute-done((bf16[6,100,400]{1,2,0:T(8,128)(2,1)S(1)}, bf16[6,100,400]{1,2,0:T(8,128)(2,1)}, u32[]{:S(2)}, u32[]{:S(2)}) %collective-permute-start.1) | collective-permute-done | bytes 480032 | tf_op jit(solution)/shard_map/ppermute | solution.py:58
  413.3 9.4 %collective-permute-done.3 = bf16[6,100,400]{1,2,0:T(8,128)(2,1)} collective-permute-done((bf16[6,100,400]{1,2,0:T(8,128)(2,1)}, bf16[6,100,400]{1,2,0:T(8,128)(2,1)}, u32[]{:S(2)}, u32[]{:S(2)}) %collective-permute-start.3) | collective-permute-done | bytes 480032 | tf_op jit(solution)/shard_map/ppermute | solution.py:58
  429.8 12.5 %collective-permute-done.5 = bf16[6,100,400]{1,2,0:T(8,128)(2,1)} collective-permute-done((bf16[6,100,400]{1,2,0:T(8,128)(2,1)}, bf16[6,100,400]{1,2,0:T(8,128)(2,1)}, u32[]{:S(2)}, u32[]{:S(2)}) %collective-permute-start.5) | collective-permute-done | bytes 480032 | tf_op jit(solution)/shard_map/ppermute | solution.py:58
  447.6 7.7 %collective-permute-done.6 = bf16[6,100,400]{1,2,0:T(8,128)(2,1)} collective-permute-done((bf16[6,100,400]{1,2,0:T(8,128)(2,1)}, bf16[6,100,400]{1,2,0:T(8,128)(2,1)}, u32[]{:S(2)}, u32[]{:S(2)}) %collective-permute-start.6) | collective-permute-done | bytes 480032 | tf_op jit(solution)/shard_map/ppermute | solution.py:58
  459.2 9.2 %all_to_all.15 = bf16[2,4,100,100]{2,0,3,1:T(2,128)(2,1)S(1)} all-to-all(bf16[2,4,100,100]{2,0,3,1:T(2,128)(2,1)S(1)} %copy.56), channel_id=1, replica_groups=mesh['pb'=8,'row'=4] {'row'}, dimensions={1} | all-to-all | bytes 320000 | tf_op jit(solution)/shard_map/all_to_all | solution.py:111
  (133 shorter events, 122.0 us)
Async XLA Ops:
  7.2 16.4 %copy-start = (s32[8]{0:T(128)S(1)}, s32[8]{0:T(128)}, u32[]{:S(2)}) copy-start(s32[8]{0:T(128)} %param.21) | copy-start | bytes 100
  7.2 17.7 %copy-start.2 = (bf16[1,20,1024]{2,1,0:T(8,128)(2,1)S(1)}, bf16[1,20,1024]{2,1,0:T(8,128)(2,1)}, u32[]{:S(2)}) copy-start(bf16[1,20,1024]{2,1,0:T(8,128)(2,1)} %param.16) | copy-start | bytes 122884
  7.2 50.4 %all-gather.2.cloned.1.call-start = ((), (), s32[]{:S(2)}) async-start(), calls=%async_computation.1 | async-start | bytes 1966080 | tf_op jit(solution)/shard_map/all_gather | solution.py:80
  22.8 12.6 %copy-start.3 = (s32[16,2]{0,1:T(2,128)S(1)}, s32[16,2]{0,1:T(2,128)}, u32[]{:S(2)}) copy-start(s32[16,2]{0,1:T(2,128)} %param.19) | copy-start | bytes 388
  22.8 13.3 %copy-start.4 = (u32[32]{0:T(128)S(1)}, u32[32]{0:T(128)}, u32[]{:S(2)}) copy-start(u32[32]{0:T(128)} %constant.159) | copy-start | bytes 388
  57.6 3.4 copy-start.1
  388.9 18.6 %collective-permute-start = (bf16[6,100,400]{1,2,0:T(8,128)(2,1)S(1)}, bf16[6,100,400]{1,2,0:T(8,128)(2,1)}, u32[]{:S(2)}, u32[]{:S(2)}) collective-permute-start(bf16[6,100,400]{1,2,0:T(8,128)(2,1)S(1)} %dynamic-slice_convert_fusion), channel_id=1, source_target_pairs={{0,28},{4,0},{8,4},{12,8},{16,12},{20,16},{24,20},{28,24},{1,29},{... | collective-permute-start | bytes 1440008 | tf_op jit(solution)/shard_map/ppermute | solution.py:60
  389.0 16.1 %collective-permute-start.1 = (bf16[6,100,400]{1,2,0:T(8,128)(2,1)S(1)}, bf16[6,100,400]{1,2,0:T(8,128)(2,1)}, u32[]{:S(2)}, u32[]{:S(2)}) collective-permute-start(bf16[6,100,400]{1,2,0:T(8,128)(2,1)S(1)} %dynamic-slice_convert_fusion), channel_id=1, source_target_pairs={{0,4},{4,8},{8,12},{12,16},{16,20},{20,24},{24,28},{28,0},{1,5},{5... | collective-permute-start | bytes 1440008 | tf_op jit(solution)/shard_map/ppermute | solution.py:58
  407.3 15.4 %collective-permute-start.3 = (bf16[6,100,400]{1,2,0:T(8,128)(2,1)}, bf16[6,100,400]{1,2,0:T(8,128)(2,1)}, u32[]{:S(2)}, u32[]{:S(2)}) collective-permute-start(bf16[6,100,400]{1,2,0:T(8,128)(2,1)} %collective-permute-done.1), channel_id=1, source_target_pairs={{0,4},{4,8},{8,12},{12,16},{16,20},{20,24},{24,28},{28,0},{1,5},{5... | collective-permute-start | bytes 1440008 | tf_op jit(solution)/shard_map/ppermute | solution.py:58
  409.7 15.2 %collective-permute-start.2 = (bf16[6,100,400]{1,2,0:T(8,128)(2,1)}, bf16[6,100,400]{1,2,0:T(8,128)(2,1)S(1)}, u32[]{:S(2)}, u32[]{:S(2)}) collective-permute-start(bf16[6,100,400]{1,2,0:T(8,128)(2,1)} %collective-permute-done), channel_id=1, source_target_pairs={{0,28},{4,0},{8,4},{12,8},{16,12},{20,16},{24,20},{28,24},{1,29},{... | collective-permute-start | bytes 1440008 | tf_op jit(solution)/shard_map/ppermute | solution.py:60
  424.9 17.4 %collective-permute-start.5 = (bf16[6,100,400]{1,2,0:T(8,128)(2,1)}, bf16[6,100,400]{1,2,0:T(8,128)(2,1)}, u32[]{:S(2)}, u32[]{:S(2)}) collective-permute-start(bf16[6,100,400]{1,2,0:T(8,128)(2,1)} %collective-permute-done.3), channel_id=1, source_target_pairs={{0,4},{4,8},{8,12},{12,16},{16,20},{20,24},{24,28},{28,0},{1,5},{5... | collective-permute-start | bytes 1440008 | tf_op jit(solution)/shard_map/ppermute | solution.py:58
  426.2 18.3 %collective-permute-start.4 = (bf16[6,100,400]{1,2,0:T(8,128)(2,1)S(1)}, bf16[6,100,400]{1,2,0:T(8,128)(2,1)}, u32[]{:S(2)}, u32[]{:S(2)}) collective-permute-start(bf16[6,100,400]{1,2,0:T(8,128)(2,1)S(1)} %collective-permute-done.2), channel_id=1, source_target_pairs={{0,28},{4,0},{8,4},{12,8},{16,12},{20,16},{24,20},{28,24},{1,29},{... | collective-permute-start | bytes 1440008 | tf_op jit(solution)/shard_map/ppermute | solution.py:60
  444.4 10.8 %collective-permute-start.6 = (bf16[6,100,400]{1,2,0:T(8,128)(2,1)}, bf16[6,100,400]{1,2,0:T(8,128)(2,1)}, u32[]{:S(2)}, u32[]{:S(2)}) collective-permute-start(bf16[6,100,400]{1,2,0:T(8,128)(2,1)} %collective-permute-done.5), channel_id=1, source_target_pairs={{0,4},{4,8},{8,12},{12,16},{16,20},{20,24},{24,28},{28,0},{1,5},{5... | collective-permute-start | bytes 1440008 | tf_op jit(solution)/shard_map/ppermute | solution.py:58
Sparse Core Ops, SparseCore 0:
  20.3 37.2 all-gather.1
